TPU v7x, 32 devices: a whole 2x2x4 slice. The times are simulated.
32 devices in a mesh: store: 8 (over y, x, core), tp: 4 (over z).
Axes of the slice: x: 2, y: 2, z: 4, core: 2. Of those that a mesh axis runs over, the one named last changes fastest.
Arguments:
- hidden: bfloat16 [8, 576, 8192], P('store', None, 'tp'), may hold values from -300 to 300
- w_query: bfloat16 [8192, 4096], P(None, 'tp'), may hold values from -0.0625 to 0.0625
- w_keyvalue: bfloat16 [8192, 1024], P('tp'), may hold values from -0.1875 to 0.1875
- passage_cache: bfloat16 [32, 4, 384, 256], P('store'), may hold values from -400 to 400
- passage_ids: int32 [8, 8], replicated, may hold values from 0 to 31, as said below
- select_index: int32 [8, 576], P('store'), may hold values from 0 to 3071, as said below
- select_count: int32 [8], P('store'), may hold values from 288 to 576, as said below
Outputs:
- context: bfloat16 [8, 576, 4096], P('store', None, 'tp')
Inputs may be any that keep to these rules, and one draw needn't show every extreme that they name: `passage_ids`: the passages of one prompt lie in distinct shards of the pool, shard = id // 4. `select_index`: all entries of a row are distinct positions of the prompt; the first select_count[p] of row p are in increasing order, the others are ignored. `select_count`: some prompt of every draw has 576 selected tokens.
All inputs are finite; a program needn't handle non-finite values.
Results may differ from a plain program's by a relative error of at most 0.04.
Values may be sent and summed in bfloat16 or wider, within the bound.
No kernel may reach another device: no remote copies, remote signals or barrier semaphores. Data moves between devices by JAX's collectives and lax.ppermute only.
A program may use at most 128 MiB of HBM per device.

v0:
```python
import jax
import jax.numpy as jnp
from jax import lax
from jax.sharding import PartitionSpec as P

D = 8192
KV_HEADS = 4
HEAD_DIM = 128
PASSAGE = 384
PASSAGES = 8
SEQ = 3072


ROPE_BASE = 1000000.0
EPSILON = 1e-06


def rotate(vectors, positions):
    half_dim = vectors.shape[-1] // 2
    frequency = ROPE_BASE ** (-(jnp.arange(half_dim, dtype=jnp.float32) * 2.0) / vectors.shape[-1])
    angles = positions.astype(jnp.float32)[..., None] * frequency
    cosine = jnp.cos(angles)
    sine_part = jnp.sin(angles)
    front_half = vectors[..., :half_dim]
    back_half = vectors[..., half_dim:]
    return jnp.concatenate(
        [front_half * cosine - back_half * sine_part, back_half * cosine + front_half * sine_part],
        axis=-1,
    )


def local(hidden, w_query, w_keyvalue, passage_cache, passage_ids, select_index, select_count):
    tp_count = lax.axis_size("tp")
    group_width = tp_count // KV_HEADS
    tp_rank = lax.axis_index("tp")
    kv_head = tp_rank // group_width
    store_rank = lax.axis_index("store")
    local_heads = w_query.shape[1] // HEAD_DIM
    row_count = hidden.shape[1]
    pool_dev = passage_cache.shape[0]
    partial_kv = jnp.dot(hidden[0], w_keyvalue, preferred_element_type=jnp.float32)
    proj_kv = lax.psum(partial_kv, "tp")
    head_kv = lax.dynamic_slice_in_dim(proj_kv, kv_head * 2 * HEAD_DIM, 2 * HEAD_DIM, 1)
    token_part = lax.all_gather(hidden, "tp", axis=2, tiled=True)[0]
    widened = token_part.astype(jnp.float32)
    running = jnp.dot(token_part, w_query, preferred_element_type=jnp.float32)
    squares = jnp.sum(widened * widened, axis=-1)
    inverse_rms = lax.rsqrt(squares / D + EPSILON)
    positions = select_index[0]
    live_count = select_count[0]
    queries = rotate(
        (running * inverse_rms[:, None]).reshape(row_count, local_heads, HEAD_DIM),
        positions[:, None],
    )
    queries = (queries * HEAD_DIM ** (-0.5)).astype(jnp.bfloat16)
    key_value = head_kv * inverse_rms[:, None]
    new_keys = rotate(key_value[:, :HEAD_DIM], positions).astype(jnp.bfloat16)
    new_values = key_value[:, HEAD_DIM:].astype(jnp.bfloat16)
    head_cache = lax.dynamic_index_in_dim(passage_cache, kv_head, 1, keepdims=False)
    owners = passage_ids // pool_dev
    local_index = passage_ids % pool_dev
    matches = owners == store_rank
    local_slot = jnp.sum(jnp.where(matches, local_index, 0), axis=1)
    present = jnp.any(matches, axis=1)
    outgoing = jnp.take(head_cache, local_slot, axis=0) * present[:, None, None].astype(
        jnp.bfloat16
    )
    incoming = lax.all_to_all(outgoing, "store", split_axis=0, concat_axis=0, tiled=True)
    my_owners = lax.dynamic_index_in_dim(owners, store_rank, 0, keepdims=False)
    fetched = jnp.take(incoming, my_owners, axis=0)
    offsets = jnp.arange(PASSAGES) * PASSAGE
    old_keys = rotate(fetched[..., :HEAD_DIM].astype(jnp.float32), offsets[:, None]).astype(
        jnp.bfloat16
    )
    old_keys = old_keys.reshape(SEQ, HEAD_DIM)
    old_values = fetched[..., HEAD_DIM:].reshape(SEQ, HEAD_DIM)
    row_ids = jnp.arange(row_count, dtype=jnp.int32)
    target = jnp.where(row_ids < live_count, positions, SEQ)
    all_keys = old_keys.at[target].set(new_keys, mode="drop")
    all_values = old_values.at[target].set(new_values, mode="drop")
    allowed = jnp.arange(SEQ, dtype=jnp.int32)[None, :] <= positions[:, None]
    scores = jnp.einsum("rgd,sd->grs", queries, all_keys, preferred_element_type=jnp.float32)
    scores = jnp.where(allowed[None], scores, -jnp.inf)
    row_max = jnp.max(scores, axis=-1, keepdims=True)
    shifted = jnp.exp(scores - row_max)
    weight = (shifted / jnp.sum(shifted, axis=-1, keepdims=True)).astype(jnp.bfloat16)
    context = jnp.einsum("grs,sd->rgd", weight, all_values, preferred_element_type=jnp.float32)
    row_live = (row_ids < live_count)[:, None, None]
    context = jnp.where(row_live, context, 0.0)
    return context.reshape(1, row_count, local_heads * HEAD_DIM).astype(jnp.bfloat16)


def solution(mesh):
    in_specs = (
        P("store", None, "tp"),
        P(None, "tp"),
        P("tp", None),
        P("store", None, None, None),
        P(),
        P("store", None),
        P("store"),
    )
    out_specs = P("store", None, "tp")
    return jax.shard_map(local, mesh=mesh, in_specs=in_specs, out_specs=out_specs, check_vma=False)
```

profile of v0, /device:TPU:6, one launch (start us, length us, event | category | flops | bytes accessed | tf_op | source)
XLA Modules:
  0.0 356.3 jit_solution(9565624965004974671)
XLA Ops:
  6.5 0.0 copy-start
  6.5 0.0 copy-start.5
  6.5 0.0 all-gather.2.cloned.1.call-start
  6.5 0.7 all-gather.2.cloned.1.call-update
  7.3 0.1 copy-done.5
  7.4 0.1 fusion.36
  7.5 0.1 fusion.29
  7.6 0.8 copy-done
  8.4 0.9 dynamic-slice_bitcast_fusion
  9.4 1.8 gather_fusion
  11.2 1.3 select_multiply_fusion
  12.5 4.2 %all-to-all-start = ((bf16[8,384,256]{2,1,0:T(8,128)(2,1)}), bf16[8,384,256]{2,1,0:T(8,128)(2,1)S(1)}, u32[]{:S(2)}, u32[]{:S(2)}) async-start(bf16[8,384,256]{2,1,0:T(8,128)(2,1)} %select_multiply_fusion), calls=%async_computation | async-start | bytes 3145728 | tf_op jit(solution)/shard_map/all_to_all | solution.py:68
  16.7 0.0 all-reduce.2.cloned.1.call-start
  16.7 8.0 %fusion.10 = f32[576,1024]{1,0:T(8,128)} fusion(bf16[2048,1024]{1,0:T(8,128)(2,1)} %param.9, bf16[1,576,2048]{2,1,0:T(8,128)(2,1)} %param.7), kind=kOutput, calls=%fused_computation.19 | convolution fusion | flops 2415919104 | bytes 8912896 | tf_op jit(solution)/shard_map/dot_general | solution.py:41
  24.7 0.0 copy-start.6
  24.7 0.0 all-reduce.2.cloned.1.call-update
  25.4 0.0 copy-done.6
  25.5 0.1 multiply_cosine_fusion.1
  25.6 2.6 iota_compare_fusion
  28.2 7.2 %all-to-all-done = bf16[8,384,256]{2,1,0:T(8,128)(2,1)S(1)} async-done(((bf16[8,384,256]{2,1,0:T(8,128)(2,1)}), bf16[8,384,256]{2,1,0:T(8,128)(2,1)S(1)}, u32[]{:S(2)}, u32[]{:S(2)}) %all-to-all-start) | async-done | bytes 1572896 | tf_op jit(solution)/shard_map/all_to_all | solution.py:68
  35.4 1.8 gather_fusion.1
  37.2 1.6 broadcast_select_fusion
  38.8 1.1 fusion.38
  39.9 0.6 subtract_convert_fusion
  40.6 1.3 pad_maximum_fusion
  41.9 135.0 %all-gather.2.cloned.1.call-done = bf16[1,576,8192]{2,1,0:T(8,128)(2,1)} async-done(((bf16[1,576,2048]{2,1,0:T(8,128)(2,1)}), bf16[1,576,8192]{2,1,0:T(8,128)(2,1)}) %all-gather.2.cloned.1.call-update) | async-done | bytes 9437200 | tf_op jit(solution)/shard_map/all_gather | solution.py:44
  176.9 0.0 copy-start.2
  176.9 5.8 %multiply_reduce_fusion = f32[576]{0:T(1024)S(1)} fusion(bf16[1,576,8192]{2,1,0:T(8,128)(2,1)} %all-gather.2.cloned.1.call-done), kind=kLoop, calls=%fused_computation.12 | loop fusion | flops 14155200 | bytes 9439488 | tf_op jit(solution)/shard_map/reduce_sum | solution.py:47
  182.6 0.6 copy-done.2
  183.3 13.6 %multiply_bitcast_fusion = f32[72,8,8,128]{3,1,2,0:T(8,128)S(1)} fusion(bf16[8192,1024]{1,0:T(8,128)(2,1)} %param.8, bf16[1,576,8192]{2,1,0:T(8,128)(2,1)S(1)} %copy-done.2, f32[576]{0:T(1024)S(1)} %add_rsqrt_fusion), kind=kOutput, calls=%fused_computation.24 | convolution fusion | flops 9664266240 | bytes 28576000 | tf_op jit(solution)/shard_map/dot_general | solution.py:46
  196.9 0.5 copy.15
  197.5 2.9 fusion.37
  200.3 0.0 copy-start.3
  200.3 71.7 %all-reduce.2.cloned.1.call-done = f32[576,1024]{1,0:T(8,128)} async-done(((f32[576,1024]{1,0:T(8,128)}), f32[576,1024]{1,0:T(8,128)}) %all-reduce.2.cloned.1.call-update) | async-done | bytes 2359312 | tf_op jit(solution)/shard_map/psum | solution.py:42
  272.1 1.2 dynamic-slice_multiply_fusion
  273.3 2.1 subtract_convert_fusion.1
  275.4 6.4 %scatter_custom_fusion = bf16[3072,128]{1,0:T(8,128)(2,1)} fusion(bf16[3072,128]{1,0:T(8,128)(2,1)} %bitcast.68, s32[576]{0:T(1024)S(1)} %fusion.32, f32[576,256]{1,0:T(8,128)S(1)} %dynamic-slice_multiply_fusion), kind=kCustom, calls=%fused_computation.43 | custom fusion | bytes 933888 | tf_op jit(solution)/shard_map/scatter | solution.py:80
  281.8 7.2 %scatter_custom_fusion.1 = bf16[3072,128]{1,0:T(8,128)(2,1)} fusion(bf16[3072,128]{1,0:T(8,128)(2,1)} %pad_maximum_fusion, s32[576]{0:T(1024)S(1)} %fusion.32, bf16[576,64]{1,0:T(8,128)(2,1)} %get-tuple-element.17, bf16[]{:T(256)} %constant.123, bf16[576,64]{1,0:T(8,128)(2,1)S(1)} %get-tuple-element.16), kind=kCustom, calls=%fused_computation.44 | custom fusion | flops 294912 | bytes 1081856 | tf_op jit(solution)/shard_map/scatter | solution.py:79
  289.0 0.0 copy-done.3
  289.0 0.0 copy-start.4
  289.0 4.7 %multiply_subtract_fusion = (f32[576,8,64]{2,0,1:T(8,128)}, f32[576,8,64]{2,0,1:T(8,128)}) fusion(f32[576,8,64]{2,1,0:T(8,128)} %get-tuple-element.11, f32[576,8,64]{2,1,0:T(8,128)S(1)} %copy-done.3, f32[576,64]{1,0:T(8,128)S(1)} %get-tuple-element.18, f32[576,64]{1,0:T(8,128)} %get-tuple-element.19), kind=kLoop, calls=%fused_computation.23 | loop fusion | flops 1769472 | bytes 5013504 | tf_op jit(solution)/shard_map/sub | solution.py:27
  293.7 0.0 copy-done.4
  293.7 28.2 %fusion.39 = (f32[8,576]{1,0:T(8,128)S(1)}, f32[8,576,3072]{2,1,0:T(8,128)}) fusion(pred[576,3072]{1,0:T(8,128)(4,1)} %iota_compare_fusion, bf16[3072,128]{1,0:T(8,128)(2,1)S(1)} %copy-done.4, f32[576,8,64]{2,0,1:T(8,128)} %get-tuple-element.9, f32[576,8,64]{2,0,1:T(8,128)} %get-tuple-element.8), kind=kOutput, calls=%fused_computation.83 | convolution fusion | flops 3668118528 | bytes 61556736 | tf_op jit(solution)/shard_map/sub | solution.py:85
  321.9 0.0 copy-start.1
  321.9 21.4 %fusion.14 = bf16[576,8,128]{2,0,1:T(8,128)(2,1)} fusion(f32[8,576,3072]{2,1,0:T(8,128)} %get-tuple-element.23, f32[8,576]{1,0:T(8,128)S(1)} %get-tuple-element.22, pred[576]{0:T(1024)(128)(4,1)S(1)} %iota_compare_fusion.1, bf16[3072,128]{1,0:T(8,128)(2,1)} %scatter_custom_fusion), kind=kOutput, calls=%fused_computation.29 | convolution fusion | flops 3653369856 | bytes 58608192 | tf_op jit(solution)/shard_map/grs,sd->rgd/dot_general | solution.py:87
  343.4 3.0 copy.12
  346.4 3.0 convert_element_type.79
  349.4 0.0 copy-done.1
  (14 shorter events, 0.1 us)
Async XLA Ops:
  6.5 1.9 copy-start
  6.5 0.8 copy-start.5
  6.5 170.3 %all-gather.2.cloned.1.call-start = ((), (), s32[]{:S(2)}) async-start(), calls=%async_computation.2 | async-start | bytes 11796480 | tf_op jit(solution)/shard_map/all_gather | solution.py:44
  12.5 22.9 %all-to-all-start = ((bf16[8,384,256]{2,1,0:T(8,128)(2,1)}), bf16[8,384,256]{2,1,0:T(8,128)(2,1)S(1)}, u32[]{:S(2)}, u32[]{:S(2)}) async-start(bf16[8,384,256]{2,1,0:T(8,128)(2,1)} %select_multiply_fusion), calls=%async_computation | async-start | bytes 3145728 | tf_op jit(solution)/shard_map/all_to_all | solution.py:68
  16.7 255.4 %all-reduce.2.cloned.1.call-start = ((), (), s32[]{:S(2)}) async-start(), calls=%async_computation.1 | async-start | bytes 4718592 | tf_op jit(solution)/shard_map/psum | solution.py:42
  24.7 0.7 copy-start.6
  176.9 6.4 %copy-start.2 = (bf16[1,576,8192]{2,1,0:T(8,128)(2,1)S(1)}, bf16[1,576,8192]{2,1,0:T(8,128)(2,1)}, u32[]{:S(2)}) copy-start(bf16[1,576,8192]{2,1,0:T(8,128)(2,1)} %all-gather.2.cloned.1.call-done) | copy-start | bytes 28311556
  200.3 88.6 %copy-start.3 = (f32[576,8,64]{2,1,0:T(8,128)S(1)}, f32[576,8,64]{2,1,0:T(8,128)}, u32[]{:S(2)}) copy-start(f32[576,8,64]{2,1,0:T(8,128)} %get-tuple-element.10) | copy-start | bytes 3538948
  289.0 4.7 %copy-start.4 = (bf16[3072,128]{1,0:T(8,128)(2,1)S(1)}, bf16[3072,128]{1,0:T(8,128)(2,1)}, u32[]{:S(2)}) copy-start(bf16[3072,128]{1,0:T(8,128)(2,1)} %scatter_custom_fusion.1) | copy-start | bytes 2359300
  321.9 27.5 %copy-start.1 = (bf16[4,4,384,256]{3,2,1,0:T(8,128)(2,1)S(1)}, bf16[4,4,384,256]{3,2,1,0:T(8,128)(2,1)}, u32[]{:S(2)}) copy-start(bf16[4,4,384,256]{3,2,1,0:T(8,128)(2,1)} %param.10) | copy-start | bytes 9437188
Sparse Core Ops, SparseCore 0:
  8.9 167.9 all-gather.1
  179.2 92.8 all-reduce.1
where the time goes:
time: 358 us; the launch traced here: 356 us
  waiting for transfers between devices  215 us (60%)
  matrix products  71.3 us (20%)
  other arithmetic  30 us (8%)
  local copies, waits for them, and re-layouts  22 us (6%)
  between operations  14.2 us (4%)
  starting transfers between devices  4.2 us (1%)
    all_gather x1, waiting for transfers between devices, local(): token_part = lax.all_gather(hidden, 'tp', axis=2, tiled=True)[0]  135 us
    psum x1, waiting for transfers between devices, local(): proj_kv = lax.psum(partial_kv, 'tp')  71.7 us
    sub x1, matrix products, local(): shifted = jnp.exp(scores - row_max)  28.2 us
    dot_general x1, matrix products, local(): jnp.einsum('grs,sd->rgd', weight, all_values, preferred_element_type=jnp....  21.4 us
    dot_general x1, matrix products, local(): running = jnp.dot(token_part, w_query, preferred_element_type=jnp.float32)  13.6 us
    dot_general x1, matrix products, local(): jnp.dot(hidden[0], w_keyvalue, preferred_element_type=jnp.float32)  7.97 us
    all_to_all x1, waiting for transfers between devices, local(): lax.all_to_all(outgoing, 'store', split_axis=0, concat_axis=0, tiled=True)  7.16 us
  transfers between devices with their start and end apart: 3, of which 3 were waited for; matrix products, arithmetic and copies ran while one was open for 12% of the time, Pallas kernels for 0%

commit v1 on v0

v1 whole, which is shorter than its diff:
```python
import functools

import jax
import jax.numpy as jnp
from jax import lax
from jax.experimental import pallas as pl
from jax.experimental.pallas import tpu as pltpu
from jax.sharding import PartitionSpec as P

KV_HEADS = 4
HEAD_DIM = 128
ROPE_BASE = 1000000.0
EPSILON = 1e-06
LOG2_E = 1.4426950408889634
MASKED = -1e30


def divisor(total, step, most):
    best = step
    for size in range(step, min(total, most) + 1, step):
        if total % size == 0:
            best = size
    return best if total % best == 0 else total


def tables(positions, scale):
    half_dim = HEAD_DIM // 2
    frequency = ROPE_BASE ** (-(jnp.arange(half_dim, dtype=jnp.float32) * 2.0) / HEAD_DIM)
    angles = positions.astype(jnp.float32)[..., None] * frequency
    cosine = jnp.cos(angles) * scale
    sine = jnp.sin(angles) * scale
    return jnp.concatenate([cosine, cosine], -1), jnp.concatenate([-sine, sine], -1)


def turned(vectors, cosine, sine):
    half_dim = HEAD_DIM // 2
    swapped = jnp.concatenate([vectors[..., half_dim:], vectors[..., :half_dim]], -1)
    return vectors * cosine + swapped * sine


def attend_kernel(
    heads, width, span, scalars, place, sums, cosine, sine, column, keys, values, out, queries
):
    first = scalars[0] + pl.program_id(0) * width
    live = jnp.clip(scalars[1] - first, 0, width)

    @pl.when(live == 0)
    def _():
        out[...] = jnp.zeros_like(out)

    @pl.when(live > 0)
    def _():
        for head in range(heads):
            part = sums[:, head * HEAD_DIM : (head + 1) * HEAD_DIM]
            spun = part * cosine[...] + pltpu.roll(part, HEAD_DIM // 2, 1) * sine[...]
            queries[head * width : (head + 1) * width, :] = spun.astype(jnp.bfloat16)
        lowest = place[first]
        highest = place[first + live - 1]
        limit = jnp.concatenate([column[...]] * heads, axis=0)

        def step(index, carry, masked):
            total, top, mass = carry
            start = pl.multiple_of(index * span, span)
            scores = lax.dot_general(
                queries[...],
                keys[pl.ds(start, span), :],
                (((1,), (1,)), ((), ())),
                preferred_element_type=jnp.float32,
            )
            if masked:
                offset = lax.broadcasted_iota(jnp.int32, scores.shape, 1)
                scores = jnp.where(offset <= limit - start, scores, MASKED)
            peak = jnp.maximum(top, jnp.max(scores, axis=1, keepdims=True))
            weight = jnp.exp2(scores - peak)
            shrink = jnp.exp2(top - peak)
            mass = mass * shrink + jnp.sum(weight, axis=1, keepdims=True)
            total = total * shrink + jnp.dot(
                weight.astype(jnp.bfloat16),
                values[pl.ds(start, span), :],
                preferred_element_type=jnp.float32,
            )
            return total, peak, mass

        carry = (
            jnp.zeros((heads * width, HEAD_DIM), jnp.float32),
            jnp.full((heads * width, 1), MASKED, jnp.float32),
            jnp.zeros((heads * width, 1), jnp.float32),
        )
        clear = (lowest + 1) // span
        carry = lax.fori_loop(0, clear, functools.partial(step, masked=False), carry)
        carry = lax.fori_loop(
            clear, highest // span + 1, functools.partial(step, masked=True), carry
        )
        total, _, mass = carry
        result = total / mass
        row = lax.broadcasted_iota(jnp.int32, (width, HEAD_DIM), 0)
        for head in range(heads):
            part = result[head * width : (head + 1) * width, :]
            out[:, head * HEAD_DIM : (head + 1) * HEAD_DIM] = jnp.where(
                row < live, part, 0.0
            ).astype(out.dtype)


def attend(sums, cosine, sine, positions, first, live_count, keys, values):
    rows, total_width = sums.shape
    heads = total_width // HEAD_DIM
    width = divisor(rows, 16, 48)
    length = keys.shape[0]
    span = divisor(length, 128, 512)
    scalars = jnp.stack([jnp.int32(first), live_count])
    whole = lambda i, *_: (0, 0)
    block = lambda i, *_: (i, 0)
    return pl.pallas_call(
        functools.partial(attend_kernel, heads, width, span),
        out_shape=jax.ShapeDtypeStruct(sums.shape, jnp.bfloat16),
        grid_spec=pltpu.PrefetchScalarGridSpec(
            num_scalar_prefetch=2,
            grid=(rows // width,),
            in_specs=[
                pl.BlockSpec((width, total_width), block),
                pl.BlockSpec((width, HEAD_DIM), block),
                pl.BlockSpec((width, HEAD_DIM), block),
                pl.BlockSpec((width, 1), block),
                pl.BlockSpec((length, HEAD_DIM), whole),
                pl.BlockSpec((length, HEAD_DIM), whole),
            ],
            out_specs=pl.BlockSpec((width, total_width), block),
            scratch_shapes=[pltpu.VMEM((heads * width, HEAD_DIM), jnp.bfloat16)],
        ),
        cost_estimate=pl.CostEstimate(
            flops=2 * rows * total_width * length,
            bytes_accessed=rows * total_width * 6 + length * HEAD_DIM * 4,
            transcendentals=rows * heads * length // 2,
        ),
    )(
        scalars,
        positions,
        sums,
        cosine[first : first + rows],
        sine[first : first + rows],
        positions[first : first + rows, None],
        keys,
        values,
    )


def fetch_passages(passage_cache, passage_ids, kv_head):
    store_rank = lax.axis_index("store")
    pool_dev, _, passage, _ = passage_cache.shape
    head_cache = lax.dynamic_index_in_dim(passage_cache, kv_head, 1, keepdims=False)
    owners = passage_ids // pool_dev
    local_index = passage_ids % pool_dev
    matches = owners == store_rank
    local_slot = jnp.sum(jnp.where(matches, local_index, 0), axis=1)
    present = jnp.any(matches, axis=1)
    outgoing = jnp.take(head_cache, local_slot, axis=0) * present[:, None, None].astype(
        jnp.bfloat16
    )
    incoming = lax.all_to_all(outgoing, "store", split_axis=0, concat_axis=0, tiled=True)
    my_owners = lax.dynamic_index_in_dim(owners, store_rank, 0, keepdims=False)
    fetched = jnp.take(incoming, my_owners, axis=0)
    passages = passage_ids.shape[1]
    cosine, sine = tables(jnp.arange(passages) * passage, 1.0)
    old_keys = turned(
        fetched[..., :HEAD_DIM].astype(jnp.float32), cosine[:, None], sine[:, None]
    ).astype(jnp.bfloat16)
    length = passages * passage
    return old_keys.reshape(length, HEAD_DIM), fetched[..., HEAD_DIM:].reshape(length, HEAD_DIM)


def blend(old_keys, old_values, head_kv, inverse_rms, positions, live_count):
    row_count = positions.shape[0]
    cosine, sine = tables(positions, inverse_rms[:, None])
    new_keys = turned(head_kv[:, :HEAD_DIM], cosine, sine).astype(jnp.bfloat16)
    new_values = (head_kv[:, HEAD_DIM:] * inverse_rms[:, None]).astype(jnp.bfloat16)
    row_ids = jnp.arange(row_count, dtype=jnp.int32)
    target = jnp.where(row_ids < live_count, positions, old_keys.shape[0])
    keys = old_keys.at[target].set(new_keys, mode="drop")
    values = old_values.at[target].set(new_values, mode="drop")
    return keys, values


def gathered(hidden, w_query, w_keyvalue, kv_head):
    partial_kv = jnp.dot(hidden, w_keyvalue, preferred_element_type=jnp.float32)
    proj_kv = lax.psum(partial_kv, "tp")
    head_kv = lax.dynamic_slice_in_dim(proj_kv, kv_head * 2 * HEAD_DIM, 2 * HEAD_DIM, 1)
    tokens = lax.all_gather(hidden, "tp", axis=1, tiled=True)
    widened = tokens.astype(jnp.float32)
    squares = jnp.sum(widened * widened, axis=-1)
    sums = jnp.dot(tokens, w_query, preferred_element_type=jnp.float32)
    return sums, head_kv, squares


def local(hidden, w_query, w_keyvalue, passage_cache, passage_ids, select_index, select_count):
    hidden = hidden[0]
    tp_count = lax.axis_size("tp")
    features = tp_count * hidden.shape[1]
    kv_head = lax.axis_index("tp") // (tp_count // KV_HEADS)
    positions = select_index[0]
    live_count = select_count[0]
    old_keys, old_values = fetch_passages(passage_cache, passage_ids, kv_head)
    sums, head_kv, squares = gathered(hidden, w_query, w_keyvalue, kv_head)
    inverse_rms = lax.rsqrt(squares / features + EPSILON)
    keys, values = blend(old_keys, old_values, head_kv, inverse_rms, positions, live_count)
    cosine, sine = tables(positions, (inverse_rms * (HEAD_DIM**-0.5 * LOG2_E))[:, None])
    context = attend(sums, cosine, sine, positions, 0, live_count, keys, values)
    return context[None]


def solution(mesh):
    in_specs = (
        P("store", None, "tp"),
        P(None, "tp"),
        P("tp", None),
        P("store", None, None, None),
        P(),
        P("store", None),
        P("store"),
    )
    out_specs = P("store", None, "tp")
    return jax.shard_map(local, mesh=mesh, in_specs=in_specs, out_specs=out_specs, check_vma=False)
```

time: 358 us -> 357 us (level)
  matrix products: 71.3 us -> 21.8 us
  Pallas kernels: 0 us -> 33.2 us
  waiting for transfers between devices: 215 us -> 239 us
  local copies, waits for them, and re-layouts: 22 us -> 10.5 us
    pallas_call x0 -> x1, Pallas kernels: none -> 33.2 us  [attend(): pl.pallas_call(functools.partial(attend_kernel, heads, width, span), out_...]
    all_gather x1, waiting for transfers between devices: 135 us -> 165 us  [gathered(): tokens = lax.all_gather(hidden, 'tp', axis=1, tiled=True)]
    sub x1 -> x0, matrix products: 28.2 us -> none  [local(): shifted = jnp.exp(scores - row_max)]
    dot_general x3 -> x2, matrix products: 43.1 us -> 21.8 us  [the longest x1 14.6 us: gathered(): sums = jnp.dot(tokens, w_query, preferred_element_type=jnp.float32)]
    psum x1, waiting for transfers between devices: 71.7 us -> 57.1 us  [gathered(): proj_kv = lax.psum(partial_kv, 'tp')]
    all_to_all x1, waiting for transfers between devices: 7.16 us -> 16.1 us  [fetch_passages(): lax.all_to_all(outgoing, 'store', split_axis=0, concat_axis=0, tiled=True)]
    scatter x1 -> x2, other arithmetic: 7.15 us -> 15 us  [the longest x1 7.66 us: blend(): keys = old_keys.at[target].set(new_keys, mode='drop')]
    scatter x1 -> x0, local copies, waits for them, and re-layouts: 6.44 us -> none  [local(): all_values = old_values.at[target].set(new_values, mode='drop')]
  transfers between devices with their start and end apart: 3 -> 3, of which waited for: 3 -> 3; matrix products, arithmetic and copies ran while one was open for 12% -> 5% of each run, Pallas kernels for 0% -> 0%
where the time goes in v1:
time: 357 us; the launch traced here: 356 us
  waiting for transfers between devices  239 us (67%)
  Pallas kernels  33.2 us (9%)
  other arithmetic  32.2 us (9%)
  matrix products  21.8 us (6%)
  between operations  14.2 us (4%)
  local copies, waits for them, and re-layouts  10.5 us (3%)
  starting transfers between devices  4.6 us (1%)
    all_gather x1, waiting for transfers between devices, gathered(): tokens = lax.all_gather(hidden, 'tp', axis=1, tiled=True)  165 us
    psum x1, waiting for transfers between devices, gathered(): proj_kv = lax.psum(partial_kv, 'tp')  57.1 us
    pallas_call x1, Pallas kernels, attend(): pl.pallas_call(functools.partial(attend_kernel, heads, width, span), out_...  33.2 us
    all_to_all x1, waiting for transfers between devices, fetch_passages(): lax.all_to_all(outgoing, 'store', split_axis=0, concat_axis=0, tiled=True)  16.1 us
    dot_general x1, matrix products, gathered(): sums = jnp.dot(tokens, w_query, preferred_element_type=jnp.float32)  14.6 us
    scatter x1, other arithmetic, blend(): keys = old_keys.at[target].set(new_keys, mode='drop')  7.66 us
    scatter x1, other arithmetic, blend(): values = old_values.at[target].set(new_values, mode='drop')  7.33 us
    dot_general x1, matrix products, gathered(): partial_kv = jnp.dot(hidden, w_keyvalue, preferred_element_type=jnp.float32)  7.17 us
  transfers between devices with their start and end apart: 3, of which 3 were waited for; matrix products, arithmetic and copies ran while one was open for 5% of the time, Pallas kernels for 0%

profile of v1, /device:TPU:6, one launch (start us, length us, event | category | flops | bytes accessed | tf_op | source)
XLA Modules:
  0.0 355.7 jit_solution(10934008180121719671)
XLA Ops:
  6.5 0.0 copy-start
  6.5 0.0 all-reduce.2.cloned.1.call-start
  6.5 7.2 %fusion.2 = f32[576,1024]{1,0:T(8,128)} fusion(bf16[2048,1024]{1,0:T(8,128)(2,1)} %param.9, bf16[1,576,2048]{2,1,0:T(8,128)(2,1)} %param.7), kind=kOutput, calls=%fused_computation.7 | convolution fusion | flops 2415919104 | bytes 8912896 | tf_op jit(solution)/shard_map/dot_general | solution.py:184
  13.7 0.0 all-reduce.2.cloned.1.call-update
  13.7 0.0 copy-start.4
  13.7 0.0 all-gather.3.cloned.1.call-start
  13.8 0.7 all-gather.3.cloned.1.call-update
  14.5 0.0 copy-done.4
  14.5 0.1 fusion.28
  14.6 0.1 fusion.21
  14.8 0.0 copy-done
  14.8 0.9 dynamic-slice_bitcast_fusion
  15.7 2.9 gather_fusion
  18.7 2.8 select_multiply_fusion
  21.4 0.0 copy-start.2
  21.4 4.6 %all-to-all-start = ((bf16[8,384,256]{2,1,0:T(8,128)(2,1)}), bf16[8,384,256]{2,1,0:T(8,128)(2,1)}, u32[]{:S(2)}, u32[]{:S(2)}) async-start(bf16[8,384,256]{2,1,0:T(8,128)(2,1)} %select_multiply_fusion), calls=%async_computation | async-start | bytes 3145728 | tf_op jit(solution)/shard_map/all_to_all | solution.py:159
  26.6 0.0 copy-done.2
  26.7 0.0 copy-start.3
  26.7 0.9 copy.8.column
  27.6 0.6 pad_add_fusion.scalars
  28.3 0.1 multiply_cosine_fusion.1
  28.4 0.1 pad_maximum_fusion.2
  28.5 16.1 %all-to-all-done = bf16[8,384,256]{2,1,0:T(8,128)(2,1)} async-done(((bf16[8,384,256]{2,1,0:T(8,128)(2,1)}), bf16[8,384,256]{2,1,0:T(8,128)(2,1)}, u32[]{:S(2)}, u32[]{:S(2)}) %all-to-all-start) | async-done | bytes 1572896 | tf_op jit(solution)/shard_map/all_to_all | solution.py:159
  44.5 3.2 gather_fusion.1
  47.7 0.0 copy-done.3
  47.7 1.6 broadcast_select_fusion
  49.4 1.2 fusion.29
  50.5 0.5 fusion.30
  51.0 1.5 fusion.5
  52.6 57.1 %all-reduce.2.cloned.1.call-done = f32[576,1024]{1,0:T(8,128)} async-done(((f32[576,1024]{1,0:T(8,128)}), f32[576,1024]{1,0:T(8,128)}) %all-reduce.2.cloned.1.call-update) | async-done | bytes 2359312 | tf_op jit(solution)/shard_map/psum | solution.py:185
  109.7 2.0 constant_dynamic-slice_fusion.1
  111.7 165.4 %all-gather.3.cloned.1.call-done = bf16[1,576,8192]{2,1,0:T(8,128)(2,1)} async-done(((bf16[1,576,2048]{2,1,0:T(8,128)(2,1)}), bf16[1,576,8192]{2,1,0:T(8,128)(2,1)}) %all-gather.3.cloned.1.call-update) | async-done | bytes 9437200 | tf_op jit(solution)/shard_map/all_gather | solution.py:187
  277.1 0.0 copy-start.1
  277.1 5.8 %multiply_reduce_fusion = f32[576]{0:T(1024)S(1)} fusion(bf16[1,576,8192]{2,1,0:T(8,128)(2,1)} %all-gather.3.cloned.1.call-done), kind=kLoop, calls=%fused_computation.4 | loop fusion | flops 14155200 | bytes 9439488 | tf_op jit(solution)/shard_map/reduce_sum | solution.py:189
  282.9 2.1 fusion.19
  285.0 1.0 pad_maximum_fusion
  286.0 0.0 copy-done.1
  286.0 14.6 %fusion.sums = f32[576,1024]{1,0:T(8,128)} fusion(bf16[8192,1024]{1,0:T(8,128)(2,1)} %param.8, bf16[1,576,8192]{2,1,0:T(8,128)(2,1)S(1)} %copy-done.1), kind=kOutput, calls=%fused_computation.5 | convolution fusion | flops 9663676416 | bytes 28573696 | tf_op jit(solution)/shard_map/dot_general | solution.py:190
  300.6 7.3 %scatter_custom_fusion.1.values = bf16[3072,128]{1,0:T(8,128)(2,1)} fusion(bf16[3072,128]{1,0:T(8,128)(2,1)} %bitcast.29, s32[576]{0:T(1024)S(1)} %fusion.24, f32[576,1024]{1,0:T(8,128)} %all-reduce.2.cloned.1.call-done, s32[]{:T(128)} %constant.100.clone.1, s32[]{:T(128)S(6)} %add.98, f32[576]{0:T(1024)S(1)} %get-tuple-element.23), kind=kCustom, calls=%fused_computation.31 | custom fusion | flops 147456 | bytes 1085956 | tf_op jit(solution)/shard_map/scatter | solution.py:179
  308.0 7.7 %scatter_custom_fusion.keys = bf16[3072,128]{1,0:T(8,128)(2,1)} fusion(bf16[3072,128]{1,0:T(8,128)(2,1)} %bitcast.28, s32[576]{0:T(1024)S(1)} %fusion.24, f32[576,1024]{1,0:T(8,128)} %all-reduce.2.cloned.1.call-done, s32[]{:T(128)} %constant.100.clone.1, s32[]{:T(128)S(6)} %select_n.103, f32[576,64]{1,0:T(8,128)} %get-tuple-element.16, f32[]{:T(128)} %constant.122, ...), kind=kCustom, calls=%fused_computation.30 | custom fusion | flops 516096 | bytes 2556932 | tf_op jit(solution)/shard_map/scatter | solution.py:178
  315.6 33.2 %shard_map.73 = bf16[576,1024]{1,0:T(8,128)(2,1)} custom-call(s32[2]{0:T(128)} %pad_add_fusion.scalars, s32[576]{0:T(1024)} %copy-done.3, f32[576,1024]{1,0:T(8,128)} %fusion.sums, f32[576,128]{1,0:T(8,128)} %get-tuple-element.28.cosine, f32[576,128]{1,0:T(8,128)} %get-tuple-element.29.sine, s32[576,1]{1,0:T(8,128)} %copy.8.column, ...), custom_call_target="tpu_custom_call" | custom-call | flops 3623878656 | bytes 5111808 | tf_op jit(solution)/shard_map/pallas_call | solution.py:113
  (13 shorter events, 0.1 us)
Async XLA Ops:
  6.5 8.3 %copy-start = (bf16[4,4,384,256]{3,2,1,0:T(8,128)(2,1)S(1)}, bf16[4,4,384,256]{3,2,1,0:T(8,128)(2,1)}, u32[]{:S(2)}) copy-start(bf16[4,4,384,256]{3,2,1,0:T(8,128)(2,1)} %param.10) | copy-start | bytes 9437188
  6.5 103.2 %all-reduce.2.cloned.1.call-start = ((), (), s32[]{:S(2)}) async-start(), calls=%async_computation.1 | async-start | bytes 4718592 | tf_op jit(solution)/shard_map/psum | solution.py:185
  13.7 0.8 copy-start.4
  13.7 263.3 %all-gather.3.cloned.1.call-start = ((), (), s32[]{:S(2)}) async-start(), calls=%async_computation.2 | async-start | bytes 11796480 | tf_op jit(solution)/shard_map/all_gather | solution.py:187
  21.4 5.2 %copy-start.2 = (s32[1,576]{1,0:T(1,128)S(1)}, s32[1,576]{1,0:T(1,128)}, u32[]{:S(2)}) copy-start(s32[1,576]{1,0:T(1,128)} %param.12) | copy-start | bytes 6916
  21.4 23.1 %all-to-all-start = ((bf16[8,384,256]{2,1,0:T(8,128)(2,1)}), bf16[8,384,256]{2,1,0:T(8,128)(2,1)}, u32[]{:S(2)}, u32[]{:S(2)}) async-start(bf16[8,384,256]{2,1,0:T(8,128)(2,1)} %select_multiply_fusion), calls=%async_computation | async-start | bytes 3145728 | tf_op jit(solution)/shard_map/all_to_all | solution.py:159
  26.7 21.1 %copy-start.3 = (s32[576]{0:T(1024)}, s32[576]{0:T(1024)S(1)}, u32[]{:S(2)}) copy-start(s32[576]{0:T(1024)S(1)} %reduce.place) | copy-start | bytes 6916
  277.1 8.9 %copy-start.1 = (bf16[1,576,8192]{2,1,0:T(8,128)(2,1)S(1)}, bf16[1,576,8192]{2,1,0:T(8,128)(2,1)}, u32[]{:S(2)}) copy-start(bf16[1,576,8192]{2,1,0:T(8,128)(2,1)} %all-gather.3.cloned.1.call-done) | copy-start | bytes 28311556
Sparse Core Ops, SparseCore 0:
  13.9 95.7 all-reduce.1
  111.3 165.7 all-gather.2
